TPU v7x, 32 devices: a whole 2x2x4 slice. The times are simulated.
32 devices in a mesh: fsdp: 4 (over z), ctx: 2 (over x), tp: 4 (over y, core).
Axes of the slice: x: 2, y: 2, z: 4, core: 2. Of those that a mesh axis runs over, the one named last changes fastest.
Arguments:
- tokens: bfloat16 [8, 1024, 1024], P('fsdp', ('ctx', 'tp')), may hold values from -6 to 6
- key_valid: int32 [8, 1024], P('fsdp'), may hold values from 0 to 1, as said below
- first_gain: bfloat16 [2, 1024], P(None, 'fsdp'), may hold values from 0.25 to 1.75
- first_shift: bfloat16 [2, 1024], P(None, 'fsdp'), may hold values from -1.75 to 1.75
- joint_weight: bfloat16 [2, 1024, 3, 1024], P(None, 'fsdp', None, 'tp'), may hold values from -0.1875 to 0.1875
- query_bias: bfloat16 [2, 16, 64], P(None, 'tp', 'fsdp'), may hold values from -3 to 3
- value_bias: bfloat16 [2, 16, 64], P(None, 'tp', 'fsdp'), may hold values from -0.625 to 0.625
- out_weight: bfloat16 [2, 1024, 1024], P(None, 'tp', 'fsdp'), may hold values from -0.75 to 0.75
- out_bias: bfloat16 [2, 1024], P(None, 'fsdp'), may hold values from -1.75 to 1.75
- second_gain: bfloat16 [2, 1024], P(None, 'fsdp'), may hold values from 0.25 to 1.75
- second_shift: bfloat16 [2, 1024], P(None, 'fsdp'), may hold values from -1.75 to 1.75
- expand_weight: bfloat16 [2, 1024, 4096], P(None, 'fsdp', 'tp'), may hold values from -0.1875 to 0.1875
- expand_bias: bfloat16 [2, 64, 64], P(None, 'tp', 'fsdp'), may hold values from -3 to 3
- reduce_weight: bfloat16 [2, 4096, 1024], P(None, 'tp', 'fsdp'), may hold values from -0.09375 to 0.09375
- reduce_bias: bfloat16 [2, 1024], P(None, 'fsdp'), may hold values from -1.75 to 1.75
- cotangent: bfloat16 [8, 1024, 1024], P('fsdp', ('ctx', 'tp')), may hold values from -6 to 6
Outputs:
- output: bfloat16 [8, 1024, 1024], P('fsdp', ('ctx', 'tp'))
- input_grad: bfloat16 [8, 1024, 1024], P('fsdp', ('ctx', 'tp'))
- grad_first_gain: float32 [2, 1024], P(None, 'fsdp')
- grad_first_shift: float32 [2, 1024], P(None, 'fsdp')
- grad_joint_weight: float32 [2, 1024, 3, 1024], P(None, 'fsdp', None, 'tp')
- grad_query_bias: float32 [2, 16, 64], P(None, 'tp', 'fsdp')
- grad_value_bias: float32 [2, 16, 64], P(None, 'tp', 'fsdp')
- grad_out_weight: float32 [2, 1024, 1024], P(None, 'tp', 'fsdp')
- grad_out_bias: float32 [2, 1024], P(None, 'fsdp')
- grad_second_gain: float32 [2, 1024], P(None, 'fsdp')
- grad_second_shift: float32 [2, 1024], P(None, 'fsdp')
- grad_expand_weight: float32 [2, 1024, 4096], P(None, 'fsdp', 'tp')
- grad_expand_bias: float32 [2, 64, 64], P(None, 'tp', 'fsdp')
- grad_reduce_weight: float32 [2, 4096, 1024], P(None, 'tp', 'fsdp')
- grad_reduce_bias: float32 [2, 1024], P(None, 'fsdp')
Inputs may be any that keep to these rules, and one draw needn't show every extreme that they name: `key_valid`: in each clip the ones form a prefix of 128 tokens or more; clip 0 has ones throughout.
All inputs are finite; a program needn't handle non-finite values.
Results may differ from a plain program's by a relative error of at most 0.02.
Values may be sent and summed in bfloat16 or wider, within the bound.
A program may use at most 256 MiB of HBM per device.

v0:
```python
import jax
import jax.numpy as jnp
from jax import lax
from jax.sharding import PartitionSpec as P

HD = 64
LAYERS = 2
MB = 2
epsilon = 1e-06
masked_score = -10000.0


def norm_rows(rows, gain, shift):
    middle = jnp.mean(rows, axis=-1, keepdims=True)
    centred = rows - middle
    spread = jnp.mean(centred * centred, axis=-1, keepdims=True)
    return centred * lax.rsqrt(spread + epsilon) * gain + shift


def exact_gelu(values):
    return jax.nn.gelu(values, approximate=False)


def dense(left, right):
    return jnp.dot(left, right, preferred_element_type=jnp.float32)


def dense_left(left, right):
    return lax.dot_general(
        left, right, (((0,), (0,)), ((), ())), preferred_element_type=jnp.float32
    )


def dense_right(left, right):
    return lax.dot_general(
        left, right, (((1,), (1,)), ((), ())), preferred_element_type=jnp.float32
    )


def head_major(rows):
    return rows.reshape(rows.shape[0], -1, HD).transpose(1, 0, 2)


def row_major(heads):
    return heads.transpose(1, 0, 2).reshape(heads.shape[1], -1)


def spread_rows(rows):
    return lax.all_gather(rows, "tp", axis=0, tiled=True)


def gather_grad(rows):
    return lax.all_gather(rows, "tp", axis=0, tiled=True)


def combine_rows(partial_value):
    return lax.psum_scatter(
        partial_value.astype(jnp.bfloat16), "tp", scatter_dimension=0, tiled=True
    ).astype(jnp.float32)


def combine_grads(partial_value):
    return lax.psum_scatter(
        partial_value.astype(jnp.bfloat16), "tp", scatter_dimension=0, tiled=True
    ).astype(jnp.float32)


def fetch(params, layer_id):
    (
        first_gain,
        first_shift,
        joint_weight,
        query_bias,
        value_bias,
        out_weight,
        out_bias,
        second_gain,
        second_shift,
        expand_weight,
        expand_bias,
        reduce_weight,
        reduce_bias,
    ) = params
    return (
        lax.all_gather(first_gain[layer_id], "fsdp", axis=0, tiled=True),
        lax.all_gather(first_shift[layer_id], "fsdp", axis=0, tiled=True),
        lax.all_gather(joint_weight[layer_id], "fsdp", axis=0, tiled=True),
        lax.all_gather(query_bias[layer_id], "fsdp", axis=1, tiled=True),
        lax.all_gather(value_bias[layer_id], "fsdp", axis=1, tiled=True),
        lax.all_gather(out_weight[layer_id], "fsdp", axis=1, tiled=True),
        lax.all_gather(out_bias[layer_id], "fsdp", axis=0, tiled=True),
        lax.all_gather(second_gain[layer_id], "fsdp", axis=0, tiled=True),
        lax.all_gather(second_shift[layer_id], "fsdp", axis=0, tiled=True),
        lax.all_gather(expand_weight[layer_id], "fsdp", axis=0, tiled=True),
        lax.all_gather(expand_bias[layer_id], "fsdp", axis=1, tiled=True),
        lax.all_gather(reduce_weight[layer_id], "fsdp", axis=1, tiled=True),
        lax.all_gather(reduce_bias[layer_id], "fsdp", axis=0, tiled=True),
    )


def attention_scores(query_heads, key_heads, key_bias):
    raw_scores = jnp.einsum(
        "hqd,hkd->hqk", query_heads, key_heads, preferred_element_type=jnp.float32
    )
    return raw_scores * HD ** (-0.5) + key_bias


def forward_layer(residual, layer_weights, key_bias):
    (
        gain_attn,
        shift_attn,
        joint_mat,
        query_add,
        value_add,
        out_mat,
        out_add,
        gain_mlp,
        shift_mlp,
        expand_mat,
        expand_add,
        reduce_mat,
        reduce_add,
    ) = layer_weights
    normed = norm_rows(residual, gain_attn.astype(jnp.float32), shift_attn.astype(jnp.float32))
    first_in = spread_rows(normed.astype(jnp.bfloat16))
    joint = jnp.einsum("nd,dce->nce", first_in, joint_mat, preferred_element_type=jnp.float32)
    queries = (joint[:, 0] + query_add.reshape(-1).astype(jnp.float32)).astype(jnp.bfloat16)
    keys_local = joint[:, 1].astype(jnp.bfloat16)
    values_local = (joint[:, 2] + value_add.reshape(-1).astype(jnp.float32)).astype(jnp.bfloat16)
    keys_all, values_all = (
        lax.all_gather(keys_local, "ctx", axis=0, tiled=True),
        lax.all_gather(values_local, "ctx", axis=0, tiled=True),
    )
    query_heads = head_major(queries)
    key_heads = head_major(keys_all)
    value_heads = head_major(values_all)
    scores = attention_scores(query_heads, key_heads, key_bias)
    row_top = jnp.max(scores, axis=-1, keepdims=True)
    exponent = jnp.exp(scores - row_top)
    row_total = jnp.sum(exponent, axis=-1, keepdims=True)
    probs_low = (exponent / row_total).astype(jnp.bfloat16)
    log_total = row_top + jnp.log(row_total)
    mixed_heads = jnp.einsum(
        "hqk,hkd->hqd", probs_low, value_heads, preferred_element_type=jnp.float32
    )
    mixed = row_major(mixed_heads.astype(jnp.bfloat16))
    middle = residual + (combine_rows(dense(mixed, out_mat)) + out_add.astype(jnp.float32))
    normed_mlp = norm_rows(middle, gain_mlp.astype(jnp.float32), shift_mlp.astype(jnp.float32))
    second_in = spread_rows(normed_mlp.astype(jnp.bfloat16))
    before = dense(second_in, expand_mat) + expand_add.reshape(-1).astype(jnp.float32)
    active = exact_gelu(before).astype(jnp.bfloat16)
    result = middle + (combine_rows(dense(active, reduce_mat)) + reduce_add.astype(jnp.float32))
    stored = (
        residual,
        first_in,
        query_heads,
        key_heads,
        value_heads,
        log_total,
        mixed,
        middle,
        second_in,
        before,
        active,
    )
    return (result, stored)


def backward_layer(carry, stored, layer_weights, key_bias):
    (
        gain_attn,
        shift_attn,
        joint_mat,
        query_add,
        value_add,
        out_mat,
        out_add,
        gain_mlp,
        shift_mlp,
        expand_mat,
        expand_add,
        reduce_mat,
        reduce_add,
    ) = layer_weights
    (
        residual,
        first_in,
        query_heads,
        key_heads,
        value_heads,
        log_total,
        mixed,
        middle,
        second_in,
        before,
        active,
    ) = stored
    low_mlp = carry.astype(jnp.bfloat16)
    mlp_rows = gather_grad(low_mlp)
    d_reduce_mat = dense_left(active, mlp_rows)
    d_reduce_add = jnp.sum(low_mlp.astype(jnp.float32), axis=0)
    d_active = dense_right(mlp_rows, reduce_mat)
    gelu_value, gelu_back = jax.vjp(exact_gelu, before)
    d_before = gelu_back(d_active)[0].astype(jnp.bfloat16)
    d_expand_add = jnp.sum(d_before.astype(jnp.float32), axis=0).reshape(expand_add.shape)
    d_expand_mat = dense_left(second_in, d_before)
    d_second = combine_grads(dense_right(d_before, expand_mat))
    norm_value, norm_back = jax.vjp(
        norm_rows, middle, gain_mlp.astype(jnp.float32), shift_mlp.astype(jnp.float32)
    )
    d_middle, d_gain_mlp, d_shift_mlp = norm_back(d_second)
    carry_mid = carry + d_middle
    low_attn = carry_mid.astype(jnp.bfloat16)
    attn_rows = gather_grad(low_attn)
    d_out_mat = dense_left(mixed, attn_rows)
    d_out_add = jnp.sum(low_attn.astype(jnp.float32), axis=0)
    d_mixed = head_major(dense_right(attn_rows, out_mat).astype(jnp.bfloat16))
    scores = attention_scores(query_heads, key_heads, key_bias)
    attn_probs = jnp.exp(scores - log_total)
    d_values = jnp.einsum(
        "hqk,hqd->hkd", attn_probs.astype(jnp.bfloat16), d_mixed, preferred_element_type=jnp.float32
    )
    d_probs = jnp.einsum("hqd,hkd->hqk", d_mixed, value_heads, preferred_element_type=jnp.float32)
    d_scores = attn_probs * (d_probs - jnp.sum(attn_probs * d_probs, axis=-1, keepdims=True))
    d_raw = (d_scores * HD ** (-0.5)).astype(jnp.bfloat16)
    d_queries = jnp.einsum("hqk,hkd->hqd", d_raw, key_heads, preferred_element_type=jnp.float32)
    d_queries = row_major(d_queries.astype(jnp.bfloat16))
    d_keys = jnp.einsum("hqk,hqd->hkd", d_raw, query_heads, preferred_element_type=jnp.float32)
    d_keys = row_major(d_keys)
    d_values = row_major(d_values)
    d_keys, d_values = (
        lax.psum_scatter(
            d_keys.astype(jnp.bfloat16), "ctx", scatter_dimension=0, tiled=True
        ).astype(jnp.float32),
        lax.psum_scatter(
            d_values.astype(jnp.bfloat16), "ctx", scatter_dimension=0, tiled=True
        ).astype(jnp.float32),
    )
    d_keys = d_keys.astype(jnp.bfloat16)
    d_values = d_values.astype(jnp.bfloat16)
    d_joint = jnp.stack((d_queries, d_keys, d_values), axis=1)
    d_joint_mat = jnp.einsum("nd,nce->dce", first_in, d_joint, preferred_element_type=jnp.float32)
    d_query_add = jnp.sum(d_queries.astype(jnp.float32), axis=0).reshape(query_add.shape)
    d_value_add = jnp.sum(d_values.astype(jnp.float32), axis=0).reshape(value_add.shape)
    d_first = combine_grads(
        jnp.einsum("nce,dce->nd", d_joint, joint_mat, preferred_element_type=jnp.float32)
    )
    first_value, first_back = jax.vjp(
        norm_rows, residual, gain_attn.astype(jnp.float32), shift_attn.astype(jnp.float32)
    )
    d_residual, d_gain_attn, d_shift_attn = first_back(d_first)
    carry_in = carry_mid + d_residual
    layer_grads = (
        d_gain_attn,
        d_shift_attn,
        d_joint_mat,
        d_query_add,
        d_value_add,
        d_out_mat,
        d_out_add,
        d_gain_mlp,
        d_shift_mlp,
        d_expand_mat,
        d_expand_add,
        d_reduce_mat,
        d_reduce_add,
    )
    return (carry_in, layer_grads)


def local(
    tokens,
    key_valid,
    first_gain,
    first_shift,
    joint_weight,
    query_bias,
    value_bias,
    out_weight,
    out_bias,
    second_gain,
    second_shift,
    expand_weight,
    expand_bias,
    reduce_weight,
    reduce_bias,
    cotangent,
):
    params = (
        first_gain,
        first_shift,
        joint_weight,
        query_bias,
        value_bias,
        out_weight,
        out_bias,
        second_gain,
        second_shift,
        expand_weight,
        expand_bias,
        reduce_weight,
        reduce_bias,
    )
    fetched = tuple((fetch(params, layer_id) for layer_id in range(LAYERS)))
    totals = [None] * LAYERS
    outputs = []
    row_grads = []
    for batch_id in range(MB):
        key_bias = jnp.where(key_valid[batch_id] == 1, 0.0, masked_score).astype(jnp.float32)
        residual = tokens[batch_id].astype(jnp.float32)
        stores = []
        for layer_id in range(LAYERS):
            residual, stored = forward_layer(residual, fetched[layer_id], key_bias)
            stores.append(stored)
        outputs.append(residual.astype(jnp.bfloat16))
        carry = cotangent[batch_id].astype(jnp.float32)
        for layer_id in reversed(range(LAYERS)):
            carry, layer_grads = backward_layer(
                carry, stores[layer_id], fetched[layer_id], key_bias
            )
            if totals[layer_id] is None:
                totals[layer_id] = layer_grads
            else:
                totals[layer_id] = tuple(
                    (old + new for old, new in zip(totals[layer_id], layer_grads))
                )
        row_grads.append(carry.astype(jnp.bfloat16))
    stacked = [
        jnp.stack([totals[layer_id][index] for layer_id in range(LAYERS)]) for index in range(13)
    ]
    shards = (
        lax.psum_scatter(
            stacked[0].astype(jnp.bfloat16), "fsdp", scatter_dimension=1, tiled=True
        ).astype(jnp.float32),
        lax.psum_scatter(
            stacked[1].astype(jnp.bfloat16), "fsdp", scatter_dimension=1, tiled=True
        ).astype(jnp.float32),
        lax.psum_scatter(
            stacked[2].astype(jnp.bfloat16), "fsdp", scatter_dimension=1, tiled=True
        ).astype(jnp.float32),
        lax.psum_scatter(
            stacked[3].astype(jnp.bfloat16), "fsdp", scatter_dimension=2, tiled=True
        ).astype(jnp.float32),
        lax.psum_scatter(
            stacked[4].astype(jnp.bfloat16), "fsdp", scatter_dimension=2, tiled=True
        ).astype(jnp.float32),
        lax.psum_scatter(
            stacked[5].astype(jnp.bfloat16), "fsdp", scatter_dimension=2, tiled=True
        ).astype(jnp.float32),
        lax.psum_scatter(
            stacked[6].astype(jnp.bfloat16), "fsdp", scatter_dimension=1, tiled=True
        ).astype(jnp.float32),
        lax.psum_scatter(
            stacked[7].astype(jnp.bfloat16), "fsdp", scatter_dimension=1, tiled=True
        ).astype(jnp.float32),
        lax.psum_scatter(
            stacked[8].astype(jnp.bfloat16), "fsdp", scatter_dimension=1, tiled=True
        ).astype(jnp.float32),
        lax.psum_scatter(
            stacked[9].astype(jnp.bfloat16), "fsdp", scatter_dimension=1, tiled=True
        ).astype(jnp.float32),
        lax.psum_scatter(
            stacked[10].astype(jnp.bfloat16), "fsdp", scatter_dimension=2, tiled=True
        ).astype(jnp.float32),
        lax.psum_scatter(
            stacked[11].astype(jnp.bfloat16), "fsdp", scatter_dimension=2, tiled=True
        ).astype(jnp.float32),
        lax.psum_scatter(
            stacked[12].astype(jnp.bfloat16), "fsdp", scatter_dimension=1, tiled=True
        ).astype(jnp.float32),
    )
    split_sums = (
        lax.psum(shards[2].astype(jnp.bfloat16), "ctx").astype(jnp.float32),
        lax.psum(shards[3].astype(jnp.bfloat16), "ctx").astype(jnp.float32),
        lax.psum(shards[4].astype(jnp.bfloat16), "ctx").astype(jnp.float32),
        lax.psum(shards[5].astype(jnp.bfloat16), "ctx").astype(jnp.float32),
        lax.psum(shards[9].astype(jnp.bfloat16), "ctx").astype(jnp.float32),
        lax.psum(shards[10].astype(jnp.bfloat16), "ctx").astype(jnp.float32),
        lax.psum(shards[11].astype(jnp.bfloat16), "ctx").astype(jnp.float32),
    )
    vector_part = lax.psum(
        (shards[0], shards[1], shards[6], shards[7], shards[8], shards[12]), ("ctx", "tp")
    )
    return (
        jnp.stack(outputs),
        jnp.stack(row_grads),
        vector_part[0],
        vector_part[1],
        split_sums[0],
        split_sums[1],
        split_sums[2],
        split_sums[3],
        vector_part[2],
        vector_part[3],
        vector_part[4],
        split_sums[4],
        split_sums[5],
        split_sums[6],
        vector_part[5],
    )


def solution(mesh):
    placed = (
        P("fsdp", ("ctx", "tp"), None),
        P("fsdp", None),
        P(None, "fsdp"),
        P(None, "fsdp"),
        P(None, "fsdp", None, "tp"),
        P(None, "tp", "fsdp"),
        P(None, "tp", "fsdp"),
        P(None, "tp", "fsdp"),
        P(None, "fsdp"),
        P(None, "fsdp"),
        P(None, "fsdp"),
        P(None, "fsdp", "tp"),
        P(None, "tp", "fsdp"),
        P(None, "tp", "fsdp"),
        P(None, "fsdp"),
        P("fsdp", ("ctx", "tp"), None),
    )
    return jax.shard_map(
        local,
        mesh=mesh,
        in_specs=placed,
        out_specs=(
            P("fsdp", ("ctx", "tp"), None),
            P("fsdp", ("ctx", "tp"), None),
            P(None, "fsdp"),
            P(None, "fsdp"),
            P(None, "fsdp", None, "tp"),
            P(None, "tp", "fsdp"),
            P(None, "tp", "fsdp"),
            P(None, "tp", "fsdp"),
            P(None, "fsdp"),
            P(None, "fsdp"),
            P(None, "fsdp"),
            P(None, "fsdp", "tp"),
            P(None, "tp", "fsdp"),
            P(None, "tp", "fsdp"),
            P(None, "fsdp"),
        ),
        check_vma=False,
    )
```

profile of v0, /device:TPU:0, one launch (start us, length us, event | category | flops | bytes accessed | tf_op | source)
XLA Modules:
  0.0 1841.4 jit_solution(5257562722936392963)
XLA Ops:
  61.3 19.5 %all-gather.6 = bf16[1,256,1024]{2,1,0:T(8,128)(2,1)S(1)} all-gather(bf16[1,256,256]{2,1,0:T(8,128)(2,1)S(1)} %get-tuple-element.130), channel_id=8, replica_groups=mesh['fsdp'=4,'ctx'=2,'tp'=4] {'fsdp'}, dimensions={2}, use_global_device_ids=true | all-gather | bytes 655360 | tf_op jit(solution)/shard_map/all_gather | solution.py:90
  132.0 15.0 reduce-scatter.56.cloned.1.call-done
  149.2 16.8 all-gather.63.cloned.1.call-done
  227.0 13.6 all-gather.11
  240.8 27.9 %all-gather.85.cloned.1.call-done = bf16[1,1024,1024]{2,1,0:T(8,128)(2,1)} async-done(((bf16[1,256,1024]{2,1,0:T(8,128)(2,1)}), bf16[1,1024,1024]{2,1,0:T(8,128)(2,1)}) %all-gather.85.cloned.1.call-update) | async-done | bytes 2097168 | tf_op jit(solution)/shard_map/all_gather | solution.py:94
  268.7 17.6 all-gather.65.cloned.1.call-done
  290.8 14.4 all-gather.57.cloned.1.call-done
  305.2 13.4 multiply_convert_fusion.7
  318.6 35.0 %all-gather.87.cloned.1.call-done = bf16[1,1024,1024]{2,1,0:T(8,128)(2,1)} async-done(((bf16[1,1024,256]{2,1,0:T(8,128)(2,1)}), bf16[1,1024,1024]{2,1,0:T(8,128)(2,1)}) %all-gather.87.cloned.1.call-update) | async-done | bytes 2097168 | tf_op jit(solution)/shard_map/all_gather | solution.py:96
  388.2 20.1 %reduce-scatter.66.cloned.1.call-done = bf16[128,1024]{1,0:T(8,128)(2,1)} async-done(((bf16[512,1024]{1,0:T(8,128)(2,1)}), bf16[128,1024]{1,0:T(8,128)(2,1)}) %reduce-scatter.66.cloned.1.call-update) | async-done | bytes 262160 | tf_op jit(solution)/shard_map/reduce_scatter | solution.py:57
  425.4 18.0 all-gather.19
  443.6 17.2 all-gather.20
  583.7 13.4 all-gather.25
  597.3 27.3 %all-gather.91.cloned.1.call-done = bf16[1,1024,1024]{2,1,0:T(8,128)(2,1)} async-done(((bf16[1,256,1024]{2,1,0:T(8,128)(2,1)}), bf16[1,1024,1024]{2,1,0:T(8,128)(2,1)}) %all-gather.91.cloned.1.call-update) | async-done | bytes 2097168 | tf_op jit(solution)/shard_map/all_gather | solution.py:94
  624.6 17.1 all-gather.69.cloned.1.call-done
  646.2 14.3 all-gather.61.cloned.1.call-done
  660.6 13.8 multiply_convert_fusion.6
  678.8 48.4 %all-gather.93.cloned.1.call-done = bf16[1,1024,1024]{2,1,0:T(8,128)(2,1)} async-done(((bf16[1,1024,256]{2,1,0:T(8,128)(2,1)}), bf16[1,1024,1024]{2,1,0:T(8,128)(2,1)}) %all-gather.93.cloned.1.call-update) | async-done | bytes 2097168 | tf_op jit(solution)/shard_map/all_gather | solution.py:96
  771.9 26.8 %reduce-scatter.72.cloned.1.call-done = bf16[128,1024]{1,0:T(8,128)(2,1)} async-done(((bf16[512,1024]{1,0:T(8,128)(2,1)}), bf16[128,1024]{1,0:T(8,128)(2,1)}) %reduce-scatter.72.cloned.1.call-update) | async-done | bytes 262160 | tf_op jit(solution)/shard_map/reduce_scatter | solution.py:63
  800.1 26.0 %reduce-scatter.62.cloned.1.call-done = bf16[128,1024]{1,0:T(8,128)(2,1)} async-done(((bf16[512,1024]{1,0:T(8,128)(2,1)}), bf16[128,1024]{1,0:T(8,128)(2,1)}) %reduce-scatter.62.cloned.1.call-update) | async-done | bytes 262160 | tf_op jit(solution)/shard_map/reduce_scatter | solution.py:57
  826.1 27.5 %reduce-scatter.70.cloned.1.call-done = bf16[128,1024]{1,0:T(8,128)(2,1)} async-done(((bf16[512,1024]{1,0:T(8,128)(2,1)}), bf16[128,1024]{1,0:T(8,128)(2,1)}) %reduce-scatter.70.cloned.1.call-update) | async-done | bytes 262160 | tf_op jit(solution)/shard_map/reduce_scatter | solution.py:57
  858.1 16.1 all-gather.77.cloned.1.call-done
  881.5 23.0 %fusion.221 = bf16[4,1024,64]{1,2,0:T(8,128)(2,1)} fusion(f32[4,512,1024]{2,1,0:T(8,128)} %fusion.467, f32[4,512,1024]{2,1,0:T(8,128)} %copy-done.4, f32[4,512]{1,0:T(4,128)S(1)} %log_add_fusion.1, f32[1024]{0:T(1024)S(1)} %bitcast.661, f32[512,4,64]{0,2,1:T(8,128)S(1)} %bitcast.579, f32[4,64]{1,0:T(4,128)S(1)} %copy.126), kind=kOutput, calls=%fused_computation.234 | convolution fusion | flops 292031488 | bytes 17839104 | tf_op jit(solution)/shard_map/hqk,hqd->hkd/dot_general | solution.py:228
  921.5 22.2 %fusion.227 = bf16[4,1024,64]{1,2,0:T(8,128)(2,1)S(1)} fusion(f32[4,512,1024]{2,1,0:T(8,128)} %fusion.465, f32[4,512,1024]{2,1,0:T(8,128)} %copy-done.3, f32[4,512]{1,0:T(4,128)S(1)} %log_add_fusion.3, f32[1024]{0:T(1024)S(1)} %bitcast.649, f32[512,4,64]{0,2,1:T(8,128)S(1)} %bitcast.577, f32[4,64]{1,0:T(4,128)S(1)} %copy.126), kind=kOutput, calls=%fused_computation.236 | convolution fusion | flops 292031488 | bytes 17839104 | tf_op jit(solution)/shard_map/hqk,hqd->hkd/dot_general | solution.py:228
  951.3 21.7 %convert_reduce_fusion.26 = (f32[4,64]{1,0:T(4,128)S(1)}, bf16[4,512,64]{1,2,0:T(8,128)(2,1)S(1)}) fusion(bf16[4,1024,64]{1,2,0:T(8,128)(2,1)S(1)} %bitcast.575, f32[4,512,1024]{2,1,0:T(8,128)} %fusion.467, f32[4,512,1024]{2,1,0:T(8,128)} %copy-done.4, f32[4,512]{1,0:T(4,128)S(1)} %log_add_fusion.1, f32[1024]{0:T(1024)S(1)} %bitcast.663), kind=kOutput, calls=%fused_computation.405 | convolution fusion | flops 291900160 | bytes 17576960 | tf_op jit(solution)/shard_map/hqk,hkd->hqd/dot_general | solution.py:226
  977.0 21.7 %convert_reduce_fusion.27 = (f32[4,64]{1,0:T(4,128)S(1)}, bf16[4,512,64]{1,2,0:T(8,128)(2,1)S(1)}) fusion(bf16[4,1024,64]{1,2,0:T(8,128)(2,1)S(1)} %bitcast.573, f32[4,512,1024]{2,1,0:T(8,128)} %fusion.465, f32[4,512,1024]{2,1,0:T(8,128)} %copy-done.3, f32[4,512]{1,0:T(4,128)S(1)} %log_add_fusion.3, f32[1024]{0:T(1024)S(1)} %bitcast.651), kind=kOutput, calls=%fused_computation.406 | convolution fusion | flops 291900160 | bytes 17576960 | tf_op jit(solution)/shard_map/hqk,hkd->hqd/dot_general | solution.py:226
  1004.4 27.6 %reduce-scatter.78.cloned.1.call-done = bf16[128,1024]{1,0:T(8,128)(2,1)} async-done(((bf16[512,1024]{1,0:T(8,128)(2,1)}), bf16[128,1024]{1,0:T(8,128)(2,1)}) %reduce-scatter.78.cloned.1.call-update) | async-done | bytes 262160 | tf_op jit(solution)/shard_map/reduce_scatter | solution.py:63
  1037.7 16.1 all-gather.79.cloned.1.call-done
  1081.1 18.7 %reduce-scatter.96.cloned.1.call-done = bf16[128,1024]{1,0:T(8,128)(2,1)} async-done(((bf16[512,1024]{1,0:T(8,128)(2,1)}), bf16[128,1024]{1,0:T(8,128)(2,1)}) %reduce-scatter.96.cloned.1.call-update) | async-done | bytes 262160 | tf_op jit(solution)/shard_map/reduce_scatter | solution.py:63
  1099.8 28.2 %reduce-scatter.80.cloned.1.call-done = bf16[128,1024]{1,0:T(8,128)(2,1)} async-done(((bf16[512,1024]{1,0:T(8,128)(2,1)}), bf16[128,1024]{1,0:T(8,128)(2,1)}) %reduce-scatter.80.cloned.1.call-update) | async-done | bytes 262160 | tf_op jit(solution)/shard_map/reduce_scatter | solution.py:63
  1135.7 14.4 all-gather.81.cloned.1.call-done
  1157.4 22.8 %fusion.218 = bf16[4,1024,64]{1,2,0:T(8,128)(2,1)} fusion(f32[4,512,1024]{2,1,0:T(8,128)} %fusion.468, f32[4,512,1024]{2,1,0:T(8,128)} %copy-done.2, f32[4,512]{1,0:T(4,128)S(1)} %log_add_fusion, f32[1024]{0:T(1024)S(1)} %bitcast.664, f32[512,4,64]{0,2,1:T(8,128)S(1)} %bitcast.569, f32[4,64]{1,0:T(4,128)S(1)} %copy-done.104), kind=kOutput, calls=%fused_computation.233 | convolution fusion | flops 292031488 | bytes 17839104 | tf_op jit(solution)/shard_map/hqk,hqd->hkd/dot_general | solution.py:228
  1196.9 22.0 %fusion.224 = bf16[4,1024,64]{1,2,0:T(8,128)(2,1)S(1)} fusion(f32[4,512,1024]{2,1,0:T(8,128)} %fusion.466, f32[4,512,1024]{2,1,0:T(8,128)} %copy-done.1, f32[4,512]{1,0:T(4,128)S(1)} %log_add_fusion.2, f32[1024]{0:T(1024)S(1)} %bitcast.652, f32[512,4,64]{0,2,1:T(8,128)S(1)} %bitcast.563, f32[4,64]{1,0:T(4,128)S(1)} %copy-done.104), kind=kOutput, calls=%fused_computation.235 | convolution fusion | flops 292031488 | bytes 17839104 | tf_op jit(solution)/shard_map/hqk,hqd->hkd/dot_general | solution.py:228
  1226.5 22.1 %convert_reduce_fusion.28 = (f32[4,64]{1,0:T(4,128)}, bf16[4,512,64]{1,2,0:T(8,128)(2,1)S(1)}) fusion(bf16[4,1024,64]{1,2,0:T(8,128)(2,1)S(1)} %bitcast.567, f32[4,512,1024]{2,1,0:T(8,128)} %fusion.468, f32[4,512,1024]{2,1,0:T(8,128)} %copy-done.2, f32[4,512]{1,0:T(4,128)S(1)} %log_add_fusion, f32[1024]{0:T(1024)S(1)} %bitcast.666), kind=kOutput, calls=%fused_computation.407 | convolution fusion | flops 291900160 | bytes 17576960 | tf_op jit(solution)/shard_map/hqk,hkd->hqd/dot_general | solution.py:226
  1252.5 22.1 %convert_reduce_fusion.29 = (f32[4,64]{1,0:T(4,128)}, bf16[4,512,64]{1,2,0:T(8,128)(2,1)S(1)}) fusion(bf16[4,1024,64]{1,2,0:T(8,128)(2,1)S(1)} %bitcast.561, f32[4,512,1024]{2,1,0:T(8,128)} %fusion.466, f32[4,512,1024]{2,1,0:T(8,128)} %copy-done.1, f32[4,512]{1,0:T(4,128)S(1)} %log_add_fusion.2, f32[1024]{0:T(1024)S(1)} %bitcast.654), kind=kOutput, calls=%fused_computation.408 | convolution fusion | flops 291900160 | bytes 17576960 | tf_op jit(solution)/shard_map/hqk,hkd->hqd/dot_general | solution.py:226
  1337.6 77.7 %reduce-scatter.110.cloned.1.call-done = bf16[2,1024,256]{2,1,0:T(8,128)(2,1)} async-done(((bf16[2,1024,1024]{2,1,0:T(8,128)(2,1)}), bf16[2,1024,256]{2,1,0:T(8,128)(2,1)}) %reduce-scatter.110.cloned.1.call-update) | async-done | bytes 1048592 | tf_op jit(solution)/shard_map/reduce_scatter | solution.py:365
  1415.3 79.5 %reduce-scatter.108.cloned.1.call-done = bf16[2,256,1024]{2,1,0:T(8,128)(2,1)} async-done(((bf16[2,1024,1024]{2,1,0:T(8,128)(2,1)}), bf16[2,256,1024]{2,1,0:T(8,128)(2,1)}) %reduce-scatter.108.cloned.1.call-update) | async-done | bytes 1048592 | tf_op jit(solution)/shard_map/reduce_scatter | solution.py:359
  1494.7 63.2 %reduce-scatter.104.cloned.1.call-done = bf16[2,256,3,256]{3,1,2,0:T(8,128)(2,1)} async-done(((bf16[2,1024,3,256]{3,1,2,0:T(8,128)(2,1)}), bf16[2,256,3,256]{3,1,2,0:T(8,128)(2,1)}) %reduce-scatter.104.cloned.1.call-update) | async-done | bytes 786448 | tf_op jit(solution)/shard_map/reduce_scatter | solution.py:338
  1559.9 19.9 %reduce-scatter.128.cloned.1.call-done = bf16[256,2]{1,0:T(8,128)(2,1)} async-done(((bf16[1024,2]{1,0:T(8,128)(2,1)}), bf16[256,2]{1,0:T(8,128)(2,1)}) %reduce-scatter.128.cloned.1.call-update) | async-done | bytes 1040
  1580.7 18.6 %reduce-scatter.126.cloned.1.call-done = bf16[16,32]{1,0:T(8,128)(2,1)} async-done(((bf16[64,32]{1,0:T(8,128)(2,1)}), bf16[16,32]{1,0:T(8,128)(2,1)}) %reduce-scatter.126.cloned.1.call-update) | async-done | bytes 1040
  1600.1 19.1 %reduce-scatter.124.cloned.1.call-done = bf16[256,2]{1,0:T(8,128)(2,1)} async-done(((bf16[1024,2]{1,0:T(8,128)(2,1)}), bf16[256,2]{1,0:T(8,128)(2,1)}) %reduce-scatter.124.cloned.1.call-update) | async-done | bytes 1040
  1620.1 19.4 %reduce-scatter.122.cloned.1.call-done = bf16[256,2]{1,0:T(8,128)(2,1)} async-done(((bf16[1024,2]{1,0:T(8,128)(2,1)}), bf16[256,2]{1,0:T(8,128)(2,1)}) %reduce-scatter.122.cloned.1.call-update) | async-done | bytes 1040
  1640.4 19.2 %reduce-scatter.120.cloned.1.call-done = bf16[256,2]{1,0:T(8,128)(2,1)} async-done(((bf16[1024,2]{1,0:T(8,128)(2,1)}), bf16[256,2]{1,0:T(8,128)(2,1)}) %reduce-scatter.120.cloned.1.call-update) | async-done | bytes 1040
  1660.6 19.1 %reduce-scatter.116.cloned.1.call-done = bf16[16,8]{1,0:T(8,128)(2,1)} async-done(((bf16[64,8]{1,0:T(8,128)(2,1)}), bf16[16,8]{1,0:T(8,128)(2,1)}) %reduce-scatter.116.cloned.1.call-update) | async-done | bytes 272
  1680.6 18.5 %reduce-scatter.118.cloned.1.call-done = bf16[16,8]{1,0:T(8,128)(2,1)} async-done(((bf16[64,8]{1,0:T(8,128)(2,1)}), bf16[16,8]{1,0:T(8,128)(2,1)}) %reduce-scatter.118.cloned.1.call-update) | async-done | bytes 272
  1720.6 19.7 %reduce-scatter.112.cloned.1.call-done = bf16[256,2]{1,0:T(8,128)(2,1)} async-done(((bf16[1024,2]{1,0:T(8,128)(2,1)}), bf16[256,2]{1,0:T(8,128)(2,1)}) %reduce-scatter.112.cloned.1.call-update) | async-done | bytes 1040
  1741.2 22.8 %all-reduce = (f32[2,256]{1,0:T(2,128)}, f32[2,256]{1,0:T(2,128)}, f32[2,256]{1,0:T(2,128)}, f32[2,256]{1,0:T(2,128)}, f32[2,256]{1,0:T(2,128)}, /*index=5*/f32[2,256]{1,0:T(2,128)}) all-reduce(bf16[2,256]{1,0:T(2,128)(2,1)S(1)} %copy.164, bf16[2,256]{1,0:T(2,128)(2,1)S(1)} %copy.166, ...), channel_id=1, replica_groups=mesh['fsdp'=4,'ctx'=2,'tp'=4] {'ctx','tp'}, use_global_device_ids=true, to_apply=%region_73.74 | all-reduce | flops 3072 | bytes 18432 | tf_op jit(solution)/shard_map/psum | solution.py:381
  1764.0 63.7 %all-reduce.5.cloned.1.call-done = (bf16[2,256,3,256]{3,1,2,0:T(8,128)(2,1)}, bf16[2,256,256]{2,1,0:T(8,128)(2,1)}, bf16[2,256,1024]{2,1,0:T(8,128)(2,1)}, bf16[2,1024,256]{2,1,0:T(8,128)(2,1)}) async-done(((bf16[2,256,3,256]{3,1,2,0:T(8,128)(2,1)}, bf16[2,256,256]{2,1,0:T(8,128)(2,1)}, bf16[2,256,1024]{2,1,0:T(8,128)(2,1)}, bf16[2,1024,256]{2,1,0:T(8,128)(2,1)}), (bf16[2,256,3,256]{3,1,2,0:T(8,128)(2,1)}, ...) | async-done | bytes 3145744 | tf_op jit(solution)/shard_map/psum | solution.py:373
  (757 shorter events, 621.2 us)
Async XLA Ops:
  7.2 73.7 %all-gather.55.cloned.1.call-start = ((), (), s32[]{:S(2)}) async-start(), calls=%async_computation.37 | async-start | bytes 1310720 | tf_op jit(solution)/shard_map/all_gather | solution.py:49
  33.4 60.4 %all-gather.83.cloned.1.call-start = ((), (), s32[]{:S(2)}) async-start(), calls=%async_computation.79 | async-start | bytes 1966080 | tf_op jit(solution)/shard_map/all_gather | solution.py:87
  34.5 112.5 %reduce-scatter.56.cloned.1.call-start = ((), (), s32[]{:S(2)}) async-start(), calls=%async_computation.38 | async-start | bytes 1310720 | tf_op jit(solution)/shard_map/reduce_scatter | solution.py:57
  149.2 71.2 %reduce-scatter.64.cloned.1.call-start = ((), (), s32[]{:S(2)}) async-start(), calls=%async_computation.46 | async-start | bytes 1310720 | tf_op jit(solution)/shard_map/reduce_scatter | solution.py:57
  195.4 73.3 %all-gather.85.cloned.1.call-start = ((), (), s32[]{:S(2)}) async-start(), calls=%async_computation.80 | async-start | bytes 2621440 | tf_op jit(solution)/shard_map/all_gather | solution.py:94
  197.7 88.6 %all-gather.65.cloned.1.call-start = ((), (), s32[]{:S(2)}) async-start(), calls=%async_computation.47 | async-start | bytes 1310720 | tf_op jit(solution)/shard_map/all_gather | solution.py:49
  225.0 80.2 %all-gather.57.cloned.1.call-start = ((), (), s32[]{:S(2)}) async-start(), calls=%async_computation.39 | async-start | bytes 1310720 | tf_op jit(solution)/shard_map/all_gather | solution.py:49
  225.7 127.9 %all-gather.87.cloned.1.call-start = ((), (), s32[]{:S(2)}) async-start(), calls=%async_computation.81 | async-start | bytes 2621440 | tf_op jit(solution)/shard_map/all_gather | solution.py:96
  226.9 161.3 %reduce-scatter.58.cloned.1.call-start = ((), (), s32[]{:S(2)}) async-start(), calls=%async_computation.40 | async-start | bytes 1310720 | tf_op jit(solution)/shard_map/reduce_scatter | solution.py:57
  361.7 99.1 %all-gather.89.cloned.1.call-start = ((), (), s32[]{:S(2)}) async-start(), calls=%async_computation.82 | async-start | bytes 1966080 | tf_op jit(solution)/shard_map/all_gather | solution.py:87
  362.7 110.7 %all-gather.67.cloned.1.call-start = ((), (), s32[]{:S(2)}) async-start(), calls=%async_computation.49 | async-start | bytes 1310720 | tf_op jit(solution)/shard_map/all_gather | solution.py:49
  411.2 80.4 %all-gather.59.cloned.1.call-start = ((), (), s32[]{:S(2)}) async-start(), calls=%async_computation.41 | async-start | bytes 1310720 | tf_op jit(solution)/shard_map/all_gather | solution.py:49
  411.8 164.8 %reduce-scatter.68.cloned.1.call-start = ((), (), s32[]{:S(2)}) async-start(), calls=%async_computation.50 | async-start | bytes 1310720 | tf_op jit(solution)/shard_map/reduce_scatter | solution.py:57
  547.9 76.7 %all-gather.91.cloned.1.call-start = ((), (), s32[]{:S(2)}) async-start(), calls=%async_computation.83 | async-start | bytes 2621440 | tf_op jit(solution)/shard_map/all_gather | solution.py:94
  548.5 93.2 %all-gather.69.cloned.1.call-start = ((), (), s32[]{:S(2)}) async-start(), calls=%async_computation.51 | async-start | bytes 1310720 | tf_op jit(solution)/shard_map/all_gather | solution.py:49
  579.4 81.2 %all-gather.61.cloned.1.call-start = ((), (), s32[]{:S(2)}) async-start(), calls=%async_computation.43 | async-start | bytes 1310720 | tf_op jit(solution)/shard_map/all_gather | solution.py:49
  580.2 98.6 %all-gather.97.cloned.1.call-start = ((), (), s32[]{:S(2)}) async-start(), calls=%async_computation.86 | async-start | bytes 1310720 | tf_op jit(solution)/shard_map/all_gather | solution.py:53
  582.1 145.1 %all-gather.93.cloned.1.call-start = ((), (), s32[]{:S(2)}) async-start(), calls=%async_computation.84 | async-start | bytes 2621440 | tf_op jit(solution)/shard_map/all_gather | solution.py:96
  582.8 160.9 %all-gather.95.cloned.1.call-start = ((), (), s32[]{:S(2)}) async-start(), calls=%async_computation.85 | async-start | bytes 1310720 | tf_op jit(solution)/shard_map/all_gather | solution.py:53
  583.6 188.3 %reduce-scatter.88.cloned.1.call-start = ((), (), s32[]{:S(2)}) async-start(), calls=%async_computation.64 | async-start | bytes 1310720 | tf_op jit(solution)/shard_map/reduce_scatter | solution.py:63
  736.3 62.4 %reduce-scatter.72.cloned.1.call-start = ((), (), s32[]{:S(2)}) async-start(), calls=%async_computation.53 | async-start | bytes 1310720 | tf_op jit(solution)/shard_map/reduce_scatter | solution.py:63
  752.3 73.9 %reduce-scatter.62.cloned.1.call-start = ((), (), s32[]{:S(2)}) async-start(), calls=%async_computation.44 | async-start | bytes 1310720 | tf_op jit(solution)/shard_map/reduce_scatter | solution.py:57
  756.7 96.9 %reduce-scatter.70.cloned.1.call-start = ((), (), s32[]{:S(2)}) async-start(), calls=%async_computation.52 | async-start | bytes 1310720 | tf_op jit(solution)/shard_map/reduce_scatter | solution.py:57
  760.9 113.2 %all-gather.77.cloned.1.call-start = ((), (), s32[]{:S(2)}) async-start(), calls=%async_computation.65 | async-start | bytes 1310720 | tf_op jit(solution)/shard_map/all_gather | solution.py:53
  858.0 115.2 %reduce-scatter.90.cloned.1.call-start = ((), (), s32[]{:S(2)}) async-start(), calls=%async_computation.66 | async-start | bytes 786432 | tf_op jit(solution)/shard_map/reduce_scatter | solution.py:232
  906.5 66.7 %reduce-scatter.92.cloned.1.call-start = ((), (), s32[]{:S(2)}) async-start(), calls=%async_computation.67 | async-start | bytes 786432 | tf_op jit(solution)/shard_map/reduce_scatter | solution.py:235
  915.1 83.7 %reduce-scatter.74.cloned.1.call-start = ((), (), s32[]{:S(2)}) async-start(), calls=%async_computation.55 | async-start | bytes 786432 | tf_op jit(solution)/shard_map/reduce_scatter | solution.py:232
  1037.5 62.4 %reduce-scatter.96.cloned.1.call-start = ((), (), s32[]{:S(2)}) async-start(), calls=%async_computation.70 | async-start | bytes 1310720 | tf_op jit(solution)/shard_map/reduce_scatter | solution.py:63
  1062.3 65.7 %reduce-scatter.80.cloned.1.call-start = ((), (), s32[]{:S(2)}) async-start(), calls=%async_computation.59 | async-start | bytes 1310720 | tf_op jit(solution)/shard_map/reduce_scatter | solution.py:63
  1081.1 69.0 %all-gather.81.cloned.1.call-start = ((), (), s32[]{:S(2)}) async-start(), calls=%async_computation.71 | async-start | bytes 1310720 | tf_op jit(solution)/shard_map/all_gather | solution.py:53
  1135.2 113.6 %reduce-scatter.98.cloned.1.call-start = ((), (), s32[]{:S(2)}) async-start(), calls=%async_computation.72 | async-start | bytes 786432 | tf_op jit(solution)/shard_map/reduce_scatter | solution.py:232
  1182.3 66.5 %reduce-scatter.100.cloned.1.call-start = ((), (), s32[]{:S(2)}) async-start(), calls=%async_computation.73 | async-start | bytes 786432 | tf_op jit(solution)/shard_map/reduce_scatter | solution.py:235
  1190.5 84.3 %reduce-scatter.82.cloned.1.call-start = ((), (), s32[]{:S(2)}) async-start(), calls=%async_computation.61 | async-start | bytes 786432 | tf_op jit(solution)/shard_map/reduce_scatter | solution.py:232
  1226.4 94.5 %reduce-scatter.102.cloned.1.call-start = ((), (), s32[]{:S(2)}) async-start(), calls=%async_computation.74 | async-start | bytes 1310720 | tf_op jit(solution)/shard_map/reduce_scatter | solution.py:63
  1252.5 68.5 %reduce-scatter.86.cloned.1.call-start = ((), (), s32[]{:S(2)}) async-start(), calls=%async_computation.63 | async-start | bytes 1310720 | tf_op jit(solution)/shard_map/reduce_scatter | solution.py:63
  1283.2 132.0 %reduce-scatter.110.cloned.1.call-start = ((), (), s32[]{:S(2)}) async-start(), calls=%async_computation.78 | async-start | bytes 5242880 | tf_op jit(solution)/shard_map/reduce_scatter | solution.py:365
  1293.4 201.3 %reduce-scatter.108.cloned.1.call-start = ((), (), s32[]{:S(2)}) async-start(), calls=%async_computation.77 | async-start | bytes 5242880 | tf_op jit(solution)/shard_map/reduce_scatter | solution.py:359
  1303.4 254.6 %reduce-scatter.104.cloned.1.call-start = ((), (), s32[]{:S(2)}) async-start(), calls=%async_computation.75 | async-start | bytes 3932160 | tf_op jit(solution)/shard_map/reduce_scatter | solution.py:338
  1312.7 267.0 %reduce-scatter.128.cloned.1.call-start = ((), (), s32[]{:S(2)}) async-start(), calls=%async_computation.95 | async-start | bytes 327680
  1314.8 284.5 %reduce-scatter.126.cloned.1.call-start = ((), (), s32[]{:S(2)}) async-start(), calls=%async_computation.94 | async-start | bytes 20480
  1315.8 303.4 %reduce-scatter.124.cloned.1.call-start = ((), (), s32[]{:S(2)}) async-start(), calls=%async_computation.93 | async-start | bytes 327680
  1316.8 322.7 %reduce-scatter.122.cloned.1.call-start = ((), (), s32[]{:S(2)}) async-start(), calls=%async_computation.92 | async-start | bytes 327680
  1317.8 341.9 %reduce-scatter.120.cloned.1.call-start = ((), (), s32[]{:S(2)}) async-start(), calls=%async_computation.91 | async-start | bytes 327680
  1318.7 361.0 %reduce-scatter.116.cloned.1.call-start = ((), (), s32[]{:S(2)}) async-start(), calls=%async_computation.89 | async-start | bytes 20480
  1319.7 379.4 %reduce-scatter.118.cloned.1.call-start = ((), (), s32[]{:S(2)}) async-start(), calls=%async_computation.90 | async-start | bytes 20480
  1320.9 398.8 %reduce-scatter.114.cloned.1.call-start = ((), (), s32[]{:S(2)}) async-start(), calls=%async_computation.88 | async-start | bytes 327680
  1325.1 415.2 %reduce-scatter.112.cloned.1.call-start = ((), (), s32[]{:S(2)}) async-start(), calls=%async_computation.87 | async-start | bytes 327680
  1326.1 501.6 %all-reduce.5.cloned.1.call-start = ((), (), s32[]{:S(2)}) async-start(), calls=%async_computation.96 | async-start | bytes 6291456 | tf_op jit(solution)/shard_map/psum | solution.py:373
  (162 other events, 3449.6 us)
Sparse Core Ops, SparseCore 0:
  52.1 41.7 all-gather.82
  121.3 25.6 reduce-scatter.55
  149.3 16.7 all-gather.62
  195.5 24.8 reduce-scatter.63
  222.4 46.2 all-gather.84
  288.5 16.7 all-gather.56
  307.4 46.2 all-gather.86
  357.6 23.1 reduce-scatter.57
  383.4 24.8 reduce-scatter.65
  410.3 44.1 all-gather.88
  456.7 16.7 all-gather.66
  474.9 16.7 all-gather.58
  523.5 24.8 reduce-scatter.67
  551.5 24.9 reduce-scatter.59
  578.5 46.1 all-gather.90
  643.8 16.7 all-gather.60
  662.0 16.7 all-gather.96
  680.9 46.2 all-gather.92
  746.3 24.8 reduce-scatter.87
  773.7 24.8 reduce-scatter.71
  801.2 24.9 reduce-scatter.61
  828.7 24.8 reduce-scatter.69
  857.4 16.7 all-gather.76
  875.7 16.7 all-gather.70
  979.3 25.0 reduce-scatter.93
  1007.1 24.8 reduce-scatter.77
  1037.0 16.7 all-gather.78
  1055.8 16.7 all-gather.72
  1074.9 24.8 reduce-scatter.95
  1103.1 24.9 reduce-scatter.79
  1133.3 16.7 all-gather.80
  1152.2 16.7 all-gather.74
  1255.3 24.8 reduce-scatter.101
  1283.3 24.9 reduce-scatter.85
  1310.4 27.1 reduce-scatter.105
  1339.8 75.4 reduce-scatter.109
  1417.4 77.2 reduce-scatter.107
  1497.1 60.7 reduce-scatter.103
  1560.1 19.5 reduce-scatter.127
  1582.0 17.1 reduce-scatter.125
  1601.4 17.7 reduce-scatter.123
  1621.5 17.9 reduce-scatter.121
  1641.8 17.7 reduce-scatter.119
  1662.5 17.1 reduce-scatter.115
  1682.0 17.0 reduce-scatter.117
  1701.8 17.8 reduce-scatter.113
  1722.4 17.7 reduce-scatter.111
  1742.7 84.8 all-reduce.4
  (12 shorter events, 178.4 us)
where the time goes:
time: 1850 us; the launch traced here: 1840 us
  waiting for transfers between devices  986 us (53%)
  matrix products  382 us (21%)
  blocking collectives  331 us (18%)
  other arithmetic  66.7 us (4%)
  local copies, waits for them, and re-layouts  54.1 us (3%)
    unnamed x69, waiting for transfers between devices  168 us
    all_gather x8, waiting for transfers between devices, spread_rows(): return lax.all_gather(rows, 'tp', axis=0, tiled=True)  106 us
    reduce_scatter x8, waiting for transfers between devices, combine_grads(): lax.psum_scatter(partial_value.astype(jnp.bfloat16), 'tp', scatter_dimens...  103 us
    reduce_scatter x8, waiting for transfers between devices, combine_rows(): lax.psum_scatter(partial_value.astype(jnp.bfloat16), 'tp', scatter_dimens...  92.7 us
    dot_general x4, matrix products, backward_layer(): jnp.einsum('hqk,hqd->hkd', d_raw, query_heads, preferred_element_type=jnp...  89.9 us
    dot_general x4, matrix products, backward_layer(): jnp.einsum('hqk,hkd->hqd', d_raw, key_heads, preferred_element_type=jnp.f...  87.6 us
    all_gather x2, waiting for transfers between devices, fetch(): lax.all_gather(reduce_weight[layer_id], 'fsdp', axis=1, tiled=True)  83.4 us
    reduce_scatter x1, waiting for transfers between devices, local(): lax.psum_scatter(stacked[9].astype(jnp.bfloat16), 'fsdp', scatter_dimensi...  79.5 us
  transfers between devices with their start and end apart: 60, of which 42 were waited for; matrix products, arithmetic and copies ran while one was open for 23% of the time, Pallas kernels for 0%

commit v1 on v0

--- a/solution.py
+++ b/solution.py
@@ -10,6 +10,18 @@
 masked_score = -10000.0
 
 
+def ring_gather(array, axis, dim):
+    ways, here, lap = (lax.axis_size(axis), lax.axis_index(axis), array.shape[dim])
+    lengths = [n * ways if d == dim else n for d, n in enumerate(array.shape)]
+    full = lax.dynamic_update_slice_in_dim(
+        jnp.zeros(lengths, array.dtype), array, here * lap, axis=dim
+    )
+    for far in range(1, ways):
+        array = lax.ppermute(array, axis, [(d, (d + 1) % ways) for d in range(ways)])
+        full = lax.dynamic_update_slice_in_dim(full, array, (here - far) % ways * lap, axis=dim)
+    return full
+
+
 def norm_rows(rows, gain, shift):
     middle = jnp.mean(rows, axis=-1, keepdims=True)
     centred = rows - middle
@@ -46,7 +58,7 @@
 
 
 def spread_rows(rows):
-    return lax.all_gather(rows, "tp", axis=0, tiled=True)
+    return ring_gather(rows, "tp", 0)
 
 
 def gather_grad(rows):

time: 1850 us -> 1750 us (0.946)
  waiting for transfers between devices: 986 us -> 844 us
  local copies, waits for them, and re-layouts: 54.1 us -> 105 us
    all_gather x8 -> x0, waiting for transfers between devices: 106 us -> none  [spread_rows(): return lax.all_gather(rows, 'tp', axis=0, tiled=True)]
    all_gather x2, waiting for transfers between devices: 55.2 us -> 17.6 us  [fetch(): lax.all_gather(expand_weight[layer_id], 'fsdp', axis=0, tiled=True)]
    ppermute x0 -> x24, waiting for transfers between devices: none -> 28.7 us  [ring_gather(): lax.ppermute(array, axis, [(d, (d + 1) % ways) for d in range(ways)])]
    ppermute x0 -> x24, local copies, waits for them, and re-layouts: none -> 20.6 us  [ring_gather(): lax.ppermute(array, axis, [(d, (d + 1) % ways) for d in range(ways)])]
    unnamed x69 -> x61, waiting for transfers between devices: 168 us -> 166 us
  transfers between devices with their start and end apart: 60 -> 76, of which waited for: 42 -> 45; matrix products, arithmetic and copies ran while one was open for 23% -> 27% of each run, Pallas kernels for 0% -> 0%
where the time goes in v1:
time: 1750 us; the launch traced here: 1740 us
  waiting for transfers between devices  844 us (48%)
  matrix products  375 us (21%)
  blocking collectives  327 us (19%)
  local copies, waits for them, and re-layouts  105 us (6%)
  other arithmetic  60.4 us (3%)
  between operations  18.4 us (1%)
    unnamed x61, waiting for transfers between devices  166 us
    reduce_scatter x8, waiting for transfers between devices, combine_grads(): lax.psum_scatter(partial_value.astype(jnp.bfloat16), 'tp', scatter_dimens...  102 us
    reduce_scatter x8, waiting for transfers between devices, combine_rows(): lax.psum_scatter(partial_value.astype(jnp.bfloat16), 'tp', scatter_dimens...  94.2 us
    dot_general x4, matrix products, backward_layer(): jnp.einsum('hqk,hkd->hqd', d_raw, key_heads, preferred_element_type=jnp.f...  88.6 us
    dot_general x4, matrix products, backward_layer(): jnp.einsum('hqk,hqd->hkd', d_raw, query_heads, preferred_element_type=jnp...  86.5 us
    reduce_scatter x1, waiting for transfers between devices, local(): lax.psum_scatter(stacked[9].astype(jnp.bfloat16), 'fsdp', scatter_dimensi...  79.6 us
    all_gather x2, waiting for transfers between devices, fetch(): lax.all_gather(reduce_weight[layer_id], 'fsdp', axis=1, tiled=True)  78.8 us
    reduce_scatter x1, waiting for transfers between devices, local(): lax.psum_scatter(stacked[11].astype(jnp.bfloat16), 'fsdp', scatter_dimens...  77.9 us
  transfers between devices with their start and end apart: 76, of which 45 were waited for; matrix products, arithmetic and copies ran while one was open for 27% of the time, Pallas kernels for 0%

profile of v1, /device:TPU:0, one launch (start us, length us, event | category | flops | bytes accessed | tf_op | source)
XLA Modules:
  0.0 1739.5 jit_solution(2099537712184992757)
XLA Ops:
  10.8 12.6 all-gather
  38.1 20.7 %all-gather.6 = bf16[1,256,1024]{2,1,0:T(8,128)(2,1)S(1)} all-gather(bf16[1,256,256]{2,1,0:T(8,128)(2,1)S(1)} %get-tuple-element.130), channel_id=8, replica_groups=mesh['fsdp'=4,'ctx'=2,'tp'=4] {'fsdp'}, dimensions={2}, use_global_device_ids=true | all-gather | bytes 655360 | tf_op jit(solution)/shard_map/all_gather | solution.py:102
  59.4 13.1 all-gather.3
  73.4 13.1 all-gather.5
  127.0 15.0 reduce-scatter.56.cloned.1.call-done
  190.2 11.1 all-gather.8
  221.6 13.6 all-gather.11
  267.8 11.7 multiply_convert_fusion.7
  279.5 31.0 %all-gather.63.cloned.1.call-done = bf16[1,1024,1024]{2,1,0:T(8,128)(2,1)} async-done(((bf16[1,1024,256]{2,1,0:T(8,128)(2,1)}), bf16[1,1024,1024]{2,1,0:T(8,128)(2,1)}) %all-gather.63.cloned.1.call-update) | async-done | bytes 2097168 | tf_op jit(solution)/shard_map/all_gather | solution.py:108
  345.2 20.4 %reduce-scatter.66.cloned.1.call-done = bf16[128,1024]{1,0:T(8,128)(2,1)} async-done(((bf16[512,1024]{1,0:T(8,128)(2,1)}), bf16[128,1024]{1,0:T(8,128)(2,1)}) %reduce-scatter.66.cloned.1.call-update) | async-done | bytes 262160 | tf_op jit(solution)/shard_map/reduce_scatter | solution.py:69
  368.0 13.2 all-gather.17
  381.4 13.9 all-gather.19
  395.5 20.2 %all-gather.20 = bf16[1,256,1024]{2,1,0:T(8,128)(2,1)S(1)} all-gather(bf16[1,256,256]{2,1,0:T(8,128)(2,1)S(1)} %copy-done.88), channel_id=22, replica_groups=mesh['fsdp'=4,'ctx'=2,'tp'=4] {'fsdp'}, dimensions={2}, use_global_device_ids=true | all-gather | bytes 655360 | tf_op jit(solution)/shard_map/all_gather | solution.py:102
  490.8 11.1 all-gather.21
  522.1 13.3 all-gather.25
  570.9 13.0 multiply_convert_fusion.6
  583.9 47.7 %all-gather.69.cloned.1.call-done = bf16[1,1024,1024]{2,1,0:T(8,128)(2,1)} async-done(((bf16[1,1024,256]{2,1,0:T(8,128)(2,1)}), bf16[1,1024,1024]{2,1,0:T(8,128)(2,1)}) %all-gather.69.cloned.1.call-update) | async-done | bytes 2097168 | tf_op jit(solution)/shard_map/all_gather | solution.py:108
  665.8 10.9 all-gather.27
  676.6 26.2 %reduce-scatter.72.cloned.1.call-done = bf16[128,1024]{1,0:T(8,128)(2,1)} async-done(((bf16[512,1024]{1,0:T(8,128)(2,1)}), bf16[128,1024]{1,0:T(8,128)(2,1)}) %reduce-scatter.72.cloned.1.call-update) | async-done | bytes 262160 | tf_op jit(solution)/shard_map/reduce_scatter | solution.py:75
  704.3 25.8 %reduce-scatter.62.cloned.1.call-done = bf16[128,1024]{1,0:T(8,128)(2,1)} async-done(((bf16[512,1024]{1,0:T(8,128)(2,1)}), bf16[128,1024]{1,0:T(8,128)(2,1)}) %reduce-scatter.62.cloned.1.call-update) | async-done | bytes 262160 | tf_op jit(solution)/shard_map/reduce_scatter | solution.py:69
  730.1 27.5 %reduce-scatter.70.cloned.1.call-done = bf16[128,1024]{1,0:T(8,128)(2,1)} async-done(((bf16[512,1024]{1,0:T(8,128)(2,1)}), bf16[128,1024]{1,0:T(8,128)(2,1)}) %reduce-scatter.70.cloned.1.call-update) | async-done | bytes 262160 | tf_op jit(solution)/shard_map/reduce_scatter | solution.py:69
  762.5 16.2 all-gather.53.cloned.1.call-done
  785.0 22.3 %fusion.221 = bf16[4,1024,64]{1,2,0:T(8,128)(2,1)S(1)} fusion(f32[4,512,1024]{2,1,0:T(8,128)} %fusion.467, f32[4,512,1024]{2,1,0:T(8,128)} %copy-done.5, f32[4,512]{1,0:T(4,128)S(1)} %log_add_fusion.1, f32[1024]{0:T(1024)S(1)} %bitcast.661, f32[512,4,64]{0,2,1:T(8,128)S(1)} %bitcast.579, f32[4,64]{1,0:T(4,128)S(1)} %copy.236), kind=kOutput, calls=%fused_computation.234 | convolution fusion | flops 292031488 | bytes 17839104 | tf_op jit(solution)/shard_map/hqk,hqd->hkd/dot_general | solution.py:240
  821.2 22.4 %fusion.227 = bf16[4,1024,64]{1,2,0:T(8,128)(2,1)S(1)} fusion(f32[4,512,1024]{2,1,0:T(8,128)} %fusion.465, f32[4,512,1024]{2,1,0:T(8,128)} %copy-done.4, f32[4,512]{1,0:T(4,128)S(1)} %log_add_fusion.3, f32[1024]{0:T(1024)S(1)} %bitcast.649, f32[512,4,64]{0,2,1:T(8,128)S(1)} %bitcast.577, f32[4,64]{1,0:T(4,128)S(1)} %copy.236), kind=kOutput, calls=%fused_computation.236 | convolution fusion | flops 292031488 | bytes 17839104 | tf_op jit(solution)/shard_map/hqk,hqd->hkd/dot_general | solution.py:240
  851.1 22.3 %convert_reduce_fusion.26 = (f32[4,64]{1,0:T(4,128)}, bf16[4,512,64]{1,2,0:T(8,128)(2,1)S(1)}) fusion(bf16[4,1024,64]{1,2,0:T(8,128)(2,1)S(1)} %bitcast.575, f32[4,512,1024]{2,1,0:T(8,128)} %fusion.467, f32[4,512,1024]{2,1,0:T(8,128)} %copy-done.5, f32[4,512]{1,0:T(4,128)S(1)} %log_add_fusion.1, f32[1024]{0:T(1024)S(1)} %bitcast.663), kind=kOutput, calls=%fused_computation.405 | convolution fusion | flops 291900160 | bytes 17576960 | tf_op jit(solution)/shard_map/hqk,hkd->hqd/dot_general | solution.py:238
  877.5 22.4 %convert_reduce_fusion.27 = (f32[4,64]{1,0:T(4,128)}, bf16[4,512,64]{1,2,0:T(8,128)(2,1)S(1)}) fusion(bf16[4,1024,64]{1,2,0:T(8,128)(2,1)S(1)} %bitcast.573, f32[4,512,1024]{2,1,0:T(8,128)} %fusion.465, f32[4,512,1024]{2,1,0:T(8,128)} %copy-done.4, f32[4,512]{1,0:T(4,128)S(1)} %log_add_fusion.3, f32[1024]{0:T(1024)S(1)} %bitcast.651), kind=kOutput, calls=%fused_computation.406 | convolution fusion | flops 291900160 | bytes 17576960 | tf_op jit(solution)/shard_map/hqk,hkd->hqd/dot_general | solution.py:238
  904.4 27.5 %reduce-scatter.78.cloned.1.call-done = bf16[128,1024]{1,0:T(8,128)(2,1)} async-done(((bf16[512,1024]{1,0:T(8,128)(2,1)}), bf16[128,1024]{1,0:T(8,128)(2,1)}) %reduce-scatter.78.cloned.1.call-update) | async-done | bytes 262160 | tf_op jit(solution)/shard_map/reduce_scatter | solution.py:75
  937.3 16.1 all-gather.55.cloned.1.call-done
  980.5 19.9 %reduce-scatter.96.cloned.1.call-done = bf16[128,1024]{1,0:T(8,128)(2,1)} async-done(((bf16[512,1024]{1,0:T(8,128)(2,1)}), bf16[128,1024]{1,0:T(8,128)(2,1)}) %reduce-scatter.96.cloned.1.call-update) | async-done | bytes 262160 | tf_op jit(solution)/shard_map/reduce_scatter | solution.py:75
  1000.4 28.0 %reduce-scatter.80.cloned.1.call-done = bf16[128,1024]{1,0:T(8,128)(2,1)} async-done(((bf16[512,1024]{1,0:T(8,128)(2,1)}), bf16[128,1024]{1,0:T(8,128)(2,1)}) %reduce-scatter.80.cloned.1.call-update) | async-done | bytes 262160 | tf_op jit(solution)/shard_map/reduce_scatter | solution.py:75
  1034.6 15.9 all-gather.57.cloned.1.call-done
  1056.9 19.0 %fusion.218 = bf16[4,1024,64]{1,2,0:T(8,128)(2,1)} fusion(f32[4,512,1024]{2,1,0:T(8,128)} %fusion.468, f32[4,512,1024]{2,1,0:T(8,128)} %copy-done.3, f32[4,512]{1,0:T(4,128)S(1)} %log_add_fusion, f32[1024]{0:T(1024)S(1)} %bitcast.664, f32[512,4,64]{0,2,1:T(8,128)} %bitcast.569, f32[4,64]{1,0:T(4,128)S(1)} %copy-done.122), kind=kOutput, calls=%fused_computation.233 | convolution fusion | flops 292031488 | bytes 17839104 | tf_op jit(solution)/shard_map/hqk,hqd->hkd/dot_general | solution.py:240
  1092.7 22.9 %fusion.224 = bf16[4,1024,64]{1,2,0:T(8,128)(2,1)} fusion(f32[4,512,1024]{2,1,0:T(8,128)} %fusion.466, f32[4,512,1024]{2,1,0:T(8,128)} %copy-done.2, f32[4,512]{1,0:T(4,128)S(1)} %log_add_fusion.2, f32[1024]{0:T(1024)S(1)} %bitcast.652, f32[512,4,64]{0,2,1:T(8,128)S(1)} %bitcast.563, f32[4,64]{1,0:T(4,128)S(1)} %copy-done.122), kind=kOutput, calls=%fused_computation.235 | convolution fusion | flops 292031488 | bytes 17839104 | tf_op jit(solution)/shard_map/hqk,hqd->hkd/dot_general | solution.py:240
  1125.9 22.2 %convert_reduce_fusion.28 = (f32[4,64]{1,0:T(4,128)S(1)}, bf16[4,512,64]{1,2,0:T(8,128)(2,1)}) fusion(bf16[4,1024,64]{1,2,0:T(8,128)(2,1)S(1)} %bitcast.567, f32[4,512,1024]{2,1,0:T(8,128)} %fusion.468, f32[4,512,1024]{2,1,0:T(8,128)} %copy-done.3, f32[4,512]{1,0:T(4,128)S(1)} %log_add_fusion, f32[1024]{0:T(1024)S(1)} %bitcast.666), kind=kOutput, calls=%fused_computation.407 | convolution fusion | flops 291900160 | bytes 17576960 | tf_op jit(solution)/shard_map/hqk,hkd->hqd/dot_general | solution.py:238
  1153.2 21.6 %convert_reduce_fusion.29 = (f32[4,64]{1,0:T(4,128)S(1)}, bf16[4,512,64]{1,2,0:T(8,128)(2,1)S(1)}) fusion(bf16[4,1024,64]{1,2,0:T(8,128)(2,1)S(1)} %bitcast.561, f32[4,512,1024]{2,1,0:T(8,128)} %fusion.466, f32[4,512,1024]{2,1,0:T(8,128)} %copy-done.2, f32[4,512]{1,0:T(4,128)S(1)} %log_add_fusion.2, f32[1024]{0:T(1024)S(1)} %bitcast.654), kind=kOutput, calls=%fused_computation.408 | convolution fusion | flops 291900160 | bytes 17576960 | tf_op jit(solution)/shard_map/hqk,hkd->hqd/dot_general | solution.py:238
  1235.5 77.9 %reduce-scatter.110.cloned.1.call-done = bf16[2,1024,256]{2,1,0:T(8,128)(2,1)} async-done(((bf16[2,1024,1024]{2,1,0:T(8,128)(2,1)}), bf16[2,1024,256]{2,1,0:T(8,128)(2,1)}) %reduce-scatter.110.cloned.1.call-update) | async-done | bytes 1048592 | tf_op jit(solution)/shard_map/reduce_scatter | solution.py:377
  1313.4 79.6 %reduce-scatter.108.cloned.1.call-done = bf16[2,256,1024]{2,1,0:T(8,128)(2,1)} async-done(((bf16[2,1024,1024]{2,1,0:T(8,128)(2,1)}), bf16[2,256,1024]{2,1,0:T(8,128)(2,1)}) %reduce-scatter.108.cloned.1.call-update) | async-done | bytes 1048592 | tf_op jit(solution)/shard_map/reduce_scatter | solution.py:371
  1393.0 63.2 %reduce-scatter.104.cloned.1.call-done = bf16[2,256,3,256]{3,1,2,0:T(8,128)(2,1)} async-done(((bf16[2,1024,3,256]{3,1,2,0:T(8,128)(2,1)}), bf16[2,256,3,256]{3,1,2,0:T(8,128)(2,1)}) %reduce-scatter.104.cloned.1.call-update) | async-done | bytes 786448 | tf_op jit(solution)/shard_map/reduce_scatter | solution.py:350
  1458.1 20.0 %reduce-scatter.128.cloned.1.call-done = bf16[256,2]{1,0:T(8,128)(2,1)} async-done(((bf16[1024,2]{1,0:T(8,128)(2,1)}), bf16[256,2]{1,0:T(8,128)(2,1)}) %reduce-scatter.128.cloned.1.call-update) | async-done | bytes 1040
  1479.0 18.5 %reduce-scatter.126.cloned.1.call-done = bf16[16,32]{1,0:T(8,128)(2,1)} async-done(((bf16[64,32]{1,0:T(8,128)(2,1)}), bf16[16,32]{1,0:T(8,128)(2,1)}) %reduce-scatter.126.cloned.1.call-update) | async-done | bytes 1040
  1498.3 19.2 %reduce-scatter.124.cloned.1.call-done = bf16[256,2]{1,0:T(8,128)(2,1)} async-done(((bf16[1024,2]{1,0:T(8,128)(2,1)}), bf16[256,2]{1,0:T(8,128)(2,1)}) %reduce-scatter.124.cloned.1.call-update) | async-done | bytes 1040
  1518.4 19.0 %reduce-scatter.122.cloned.1.call-done = bf16[256,2]{1,0:T(8,128)(2,1)} async-done(((bf16[1024,2]{1,0:T(8,128)(2,1)}), bf16[256,2]{1,0:T(8,128)(2,1)}) %reduce-scatter.122.cloned.1.call-update) | async-done | bytes 1040
  1538.4 19.9 %reduce-scatter.120.cloned.1.call-done = bf16[256,2]{1,0:T(8,128)(2,1)} async-done(((bf16[1024,2]{1,0:T(8,128)(2,1)}), bf16[256,2]{1,0:T(8,128)(2,1)}) %reduce-scatter.120.cloned.1.call-update) | async-done | bytes 1040
  1559.2 18.9 %reduce-scatter.116.cloned.1.call-done = bf16[16,8]{1,0:T(8,128)(2,1)} async-done(((bf16[64,8]{1,0:T(8,128)(2,1)}), bf16[16,8]{1,0:T(8,128)(2,1)}) %reduce-scatter.116.cloned.1.call-update) | async-done | bytes 272
  1579.0 18.4 %reduce-scatter.118.cloned.1.call-done = bf16[16,8]{1,0:T(8,128)(2,1)} async-done(((bf16[64,8]{1,0:T(8,128)(2,1)}), bf16[16,8]{1,0:T(8,128)(2,1)}) %reduce-scatter.118.cloned.1.call-update) | async-done | bytes 272
  1618.9 19.8 %reduce-scatter.112.cloned.1.call-done = bf16[256,2]{1,0:T(8,128)(2,1)} async-done(((bf16[1024,2]{1,0:T(8,128)(2,1)}), bf16[256,2]{1,0:T(8,128)(2,1)}) %reduce-scatter.112.cloned.1.call-update) | async-done | bytes 1040
  1639.6 22.8 %all-reduce = (f32[2,256]{1,0:T(2,128)}, f32[2,256]{1,0:T(2,128)}, f32[2,256]{1,0:T(2,128)}, f32[2,256]{1,0:T(2,128)}, f32[2,256]{1,0:T(2,128)}, /*index=5*/f32[2,256]{1,0:T(2,128)}) all-reduce(bf16[2,256]{1,0:T(2,128)(2,1)S(1)} %copy.292, bf16[2,256]{1,0:T(2,128)(2,1)S(1)} %copy.294, ...), channel_id=1, replica_groups=mesh['fsdp'=4,'ctx'=2,'tp'=4] {'ctx','tp'}, use_global_device_ids=true, to_apply=%region_73.74 | all-reduce | flops 3072 | bytes 18432 | tf_op jit(solution)/shard_map/psum | solution.py:393
  1662.4 63.6 %all-reduce.5.cloned.1.call-done = (bf16[2,256,3,256]{3,1,2,0:T(8,128)(2,1)}, bf16[2,256,256]{2,1,0:T(8,128)(2,1)}, bf16[2,256,1024]{2,1,0:T(8,128)(2,1)}, bf16[2,1024,256]{2,1,0:T(8,128)(2,1)}) async-done(((bf16[2,256,3,256]{3,1,2,0:T(8,128)(2,1)}, bf16[2,256,256]{2,1,0:T(8,128)(2,1)}, bf16[2,256,1024]{2,1,0:T(8,128)(2,1)}, bf16[2,1024,256]{2,1,0:T(8,128)(2,1)}), (bf16[2,256,3,256]{3,1,2,0:T(8,128)(2,1)}, ...) | async-done | bytes 3145744 | tf_op jit(solution)/shard_map/psum | solution.py:385
  (909 shorter events, 576.4 us)
Async XLA Ops:
  7.2 81.8 %all-gather.59.cloned.1.call-start = ((), (), s32[]{:S(2)}) async-start(), calls=%async_computation.71 | async-start | bytes 1966080 | tf_op jit(solution)/shard_map/all_gather | solution.py:99
  9.5 132.5 %reduce-scatter.56.cloned.1.call-start = ((), (), s32[]{:S(2)}) async-start(), calls=%async_computation.37 | async-start | bytes 1310720 | tf_op jit(solution)/shard_map/reduce_scatter | solution.py:69
  116.9 98.2 %reduce-scatter.64.cloned.1.call-start = ((), (), s32[]{:S(2)}) async-start(), calls=%async_computation.41 | async-start | bytes 1310720 | tf_op jit(solution)/shard_map/reduce_scatter | solution.py:69
  188.5 74.9 %all-gather.61.cloned.1.call-start = ((), (), s32[]{:S(2)}) async-start(), calls=%async_computation.72 | async-start | bytes 2621440 | tf_op jit(solution)/shard_map/all_gather | solution.py:106
  189.6 121.0 %all-gather.63.cloned.1.call-start = ((), (), s32[]{:S(2)}) async-start(), calls=%async_computation.73 | async-start | bytes 2621440 | tf_op jit(solution)/shard_map/all_gather | solution.py:108
  220.4 124.8 %reduce-scatter.58.cloned.1.call-start = ((), (), s32[]{:S(2)}) async-start(), calls=%async_computation.38 | async-start | bytes 1310720 | tf_op jit(solution)/shard_map/reduce_scatter | solution.py:69
  318.7 110.4 %all-gather.65.cloned.1.call-start = ((), (), s32[]{:S(2)}) async-start(), calls=%async_computation.74 | async-start | bytes 1966080 | tf_op jit(solution)/shard_map/all_gather | solution.py:99
  319.7 199.4 %reduce-scatter.68.cloned.1.call-start = ((), (), s32[]{:S(2)}) async-start(), calls=%async_computation.43 | async-start | bytes 1310720 | tf_op jit(solution)/shard_map/reduce_scatter | solution.py:69
  464.5 54.6 %reduce-scatter.60.cloned.1.call-start = ((), (), s32[]{:S(2)}) async-start(), calls=%async_computation.39 | async-start | bytes 1310720 | tf_op jit(solution)/shard_map/reduce_scatter | solution.py:69
  488.4 77.8 %all-gather.67.cloned.1.call-start = ((), (), s32[]{:S(2)}) async-start(), calls=%async_computation.75 | async-start | bytes 2621440 | tf_op jit(solution)/shard_map/all_gather | solution.py:106
  489.1 94.8 %all-gather.73.cloned.1.call-start = ((), (), s32[]{:S(2)}) async-start(), calls=%async_computation.78 | async-start | bytes 1310720 | tf_op jit(solution)/shard_map/all_gather | solution.py:65
  490.0 141.6 %all-gather.69.cloned.1.call-start = ((), (), s32[]{:S(2)}) async-start(), calls=%async_computation.76 | async-start | bytes 2621440 | tf_op jit(solution)/shard_map/all_gather | solution.py:108
  490.8 157.3 %all-gather.71.cloned.1.call-start = ((), (), s32[]{:S(2)}) async-start(), calls=%async_computation.77 | async-start | bytes 1310720 | tf_op jit(solution)/shard_map/all_gather | solution.py:65
  521.9 154.7 %reduce-scatter.88.cloned.1.call-start = ((), (), s32[]{:S(2)}) async-start(), calls=%async_computation.56 | async-start | bytes 1310720 | tf_op jit(solution)/shard_map/reduce_scatter | solution.py:75
  640.2 62.6 %reduce-scatter.72.cloned.1.call-start = ((), (), s32[]{:S(2)}) async-start(), calls=%async_computation.45 | async-start | bytes 1310720 | tf_op jit(solution)/shard_map/reduce_scatter | solution.py:75
  656.6 73.5 %reduce-scatter.62.cloned.1.call-start = ((), (), s32[]{:S(2)}) async-start(), calls=%async_computation.40 | async-start | bytes 1310720 | tf_op jit(solution)/shard_map/reduce_scatter | solution.py:69
  661.1 96.5 %reduce-scatter.70.cloned.1.call-start = ((), (), s32[]{:S(2)}) async-start(), calls=%async_computation.44 | async-start | bytes 1310720 | tf_op jit(solution)/shard_map/reduce_scatter | solution.py:69
  665.7 113.0 %all-gather.53.cloned.1.call-start = ((), (), s32[]{:S(2)}) async-start(), calls=%async_computation.57 | async-start | bytes 1310720 | tf_op jit(solution)/shard_map/all_gather | solution.py:65
  761.9 53.1 %all-gather.47.cloned.1.call-start = ((), (), s32[]{:S(2)}) async-start(), calls=%async_computation.46 | async-start | bytes 1310720 | tf_op jit(solution)/shard_map/all_gather | solution.py:65
  762.5 111.1 %reduce-scatter.90.cloned.1.call-start = ((), (), s32[]{:S(2)}) async-start(), calls=%async_computation.58 | async-start | bytes 786432 | tf_op jit(solution)/shard_map/reduce_scatter | solution.py:244
  808.4 65.2 %reduce-scatter.92.cloned.1.call-start = ((), (), s32[]{:S(2)}) async-start(), calls=%async_computation.59 | async-start | bytes 786432 | tf_op jit(solution)/shard_map/reduce_scatter | solution.py:247
  814.7 85.4 %reduce-scatter.74.cloned.1.call-start = ((), (), s32[]{:S(2)}) async-start(), calls=%async_computation.47 | async-start | bytes 786432 | tf_op jit(solution)/shard_map/reduce_scatter | solution.py:244
  844.6 55.5 %reduce-scatter.76.cloned.1.call-start = ((), (), s32[]{:S(2)}) async-start(), calls=%async_computation.48 | async-start | bytes 786432 | tf_op jit(solution)/shard_map/reduce_scatter | solution.py:247
  851.0 53.4 %reduce-scatter.94.cloned.1.call-start = ((), (), s32[]{:S(2)}) async-start(), calls=%async_computation.60 | async-start | bytes 1310720 | tf_op jit(solution)/shard_map/reduce_scatter | solution.py:75
  877.2 54.7 %reduce-scatter.78.cloned.1.call-start = ((), (), s32[]{:S(2)}) async-start(), calls=%async_computation.49 | async-start | bytes 1310720 | tf_op jit(solution)/shard_map/reduce_scatter | solution.py:75
  937.3 63.0 %reduce-scatter.96.cloned.1.call-start = ((), (), s32[]{:S(2)}) async-start(), calls=%async_computation.62 | async-start | bytes 1310720 | tf_op jit(solution)/shard_map/reduce_scatter | solution.py:75
  962.0 66.4 %reduce-scatter.80.cloned.1.call-start = ((), (), s32[]{:S(2)}) async-start(), calls=%async_computation.51 | async-start | bytes 1310720 | tf_op jit(solution)/shard_map/reduce_scatter | solution.py:75
  980.0 70.5 %all-gather.57.cloned.1.call-start = ((), (), s32[]{:S(2)}) async-start(), calls=%async_computation.63 | async-start | bytes 1310720 | tf_op jit(solution)/shard_map/all_gather | solution.py:65
  1034.5 114.7 %reduce-scatter.98.cloned.1.call-start = ((), (), s32[]{:S(2)}) async-start(), calls=%async_computation.64 | async-start | bytes 786432 | tf_op jit(solution)/shard_map/reduce_scatter | solution.py:244
  1077.9 71.3 %reduce-scatter.100.cloned.1.call-start = ((), (), s32[]{:S(2)}) async-start(), calls=%async_computation.65 | async-start | bytes 786432 | tf_op jit(solution)/shard_map/reduce_scatter | solution.py:247
  1086.1 88.9 %reduce-scatter.82.cloned.1.call-start = ((), (), s32[]{:S(2)}) async-start(), calls=%async_computation.53 | async-start | bytes 786432 | tf_op jit(solution)/shard_map/reduce_scatter | solution.py:244
  1117.7 57.4 %reduce-scatter.84.cloned.1.call-start = ((), (), s32[]{:S(2)}) async-start(), calls=%async_computation.54 | async-start | bytes 786432 | tf_op jit(solution)/shard_map/reduce_scatter | solution.py:247
  1125.8 98.7 %reduce-scatter.102.cloned.1.call-start = ((), (), s32[]{:S(2)}) async-start(), calls=%async_computation.66 | async-start | bytes 1310720 | tf_op jit(solution)/shard_map/reduce_scatter | solution.py:75
  1152.9 71.7 %reduce-scatter.86.cloned.1.call-start = ((), (), s32[]{:S(2)}) async-start(), calls=%async_computation.55 | async-start | bytes 1310720 | tf_op jit(solution)/shard_map/reduce_scatter | solution.py:75
  1178.7 56.8 %reduce-scatter.106.cloned.1.call-start = ((), (), s32[]{:S(2)}) async-start(), calls=%async_computation.68 | async-start | bytes 1310720 | tf_op jit(solution)/shard_map/reduce_scatter | solution.py:359
  1184.1 129.2 %reduce-scatter.110.cloned.1.call-start = ((), (), s32[]{:S(2)}) async-start(), calls=%async_computation.70 | async-start | bytes 5242880 | tf_op jit(solution)/shard_map/reduce_scatter | solution.py:377
  1194.2 198.7 %reduce-scatter.108.cloned.1.call-start = ((), (), s32[]{:S(2)}) async-start(), calls=%async_computation.69 | async-start | bytes 5242880 | tf_op jit(solution)/shard_map/reduce_scatter | solution.py:371
  1205.4 250.8 %reduce-scatter.104.cloned.1.call-start = ((), (), s32[]{:S(2)}) async-start(), calls=%async_computation.67 | async-start | bytes 3932160 | tf_op jit(solution)/shard_map/reduce_scatter | solution.py:350
  1216.5 261.6 %reduce-scatter.128.cloned.1.call-start = ((), (), s32[]{:S(2)}) async-start(), calls=%async_computation.87 | async-start | bytes 327680
  1218.4 279.1 %reduce-scatter.126.cloned.1.call-start = ((), (), s32[]{:S(2)}) async-start(), calls=%async_computation.86 | async-start | bytes 20480
  1219.4 298.1 %reduce-scatter.124.cloned.1.call-start = ((), (), s32[]{:S(2)}) async-start(), calls=%async_computation.85 | async-start | bytes 327680
  1220.4 317.1 %reduce-scatter.122.cloned.1.call-start = ((), (), s32[]{:S(2)}) async-start(), calls=%async_computation.84 | async-start | bytes 327680
  1221.4 336.9 %reduce-scatter.120.cloned.1.call-start = ((), (), s32[]{:S(2)}) async-start(), calls=%async_computation.83 | async-start | bytes 327680
  1222.4 355.7 %reduce-scatter.116.cloned.1.call-start = ((), (), s32[]{:S(2)}) async-start(), calls=%async_computation.81 | async-start | bytes 20480
  1223.3 374.1 %reduce-scatter.118.cloned.1.call-start = ((), (), s32[]{:S(2)}) async-start(), calls=%async_computation.82 | async-start | bytes 20480
  1224.5 393.5 %reduce-scatter.114.cloned.1.call-start = ((), (), s32[]{:S(2)}) async-start(), calls=%async_computation.80 | async-start | bytes 327680
  1228.7 410.0 %reduce-scatter.112.cloned.1.call-start = ((), (), s32[]{:S(2)}) async-start(), calls=%async_computation.79 | async-start | bytes 327680
  1229.7 496.3 %all-reduce.5.cloned.1.call-start = ((), (), s32[]{:S(2)}) async-start(), calls=%async_computation.88 | async-start | bytes 6291456 | tf_op jit(solution)/shard_map/psum | solution.py:385
  (206 other events, 3570.1 us)
Sparse Core Ops, SparseCore 0:
  10.2 48.8 all-gather.58
  117.0 24.9 reduce-scatter.55
  188.6 26.4 reduce-scatter.63
  217.1 46.2 all-gather.60
  265.3 45.1 all-gather.62
  314.9 23.1 reduce-scatter.57
  340.8 24.8 reduce-scatter.65
  367.8 45.2 all-gather.64
  464.6 24.9 reduce-scatter.67
  492.8 24.8 reduce-scatter.59
  519.8 46.3 all-gather.66
  567.6 15.5 all-gather.72
  585.4 46.2 all-gather.68
  633.1 14.9 all-gather.70
  650.4 24.8 reduce-scatter.87
  677.9 24.8 reduce-scatter.71
  705.2 24.8 reduce-scatter.61
  732.7 24.8 reduce-scatter.69
  762.0 16.7 all-gather.52
  780.7 16.7 all-gather.46
  844.7 14.6 reduce-scatter.73
  862.2 14.5 reduce-scatter.75
  879.3 25.0 reduce-scatter.93
  906.9 24.9 reduce-scatter.77
  936.7 16.7 all-gather.54
  955.6 16.7 all-gather.48
  975.4 24.8 reduce-scatter.95
  1003.5 24.8 reduce-scatter.79
  1033.7 16.7 all-gather.56
  1052.6 16.7 all-gather.50
  1078.0 14.5 reduce-scatter.97
  1117.8 14.6 reduce-scatter.81
  1153.0 24.9 reduce-scatter.101
  1181.2 24.8 reduce-scatter.85
  1208.3 27.1 reduce-scatter.105
  1237.9 75.4 reduce-scatter.109
  1315.7 77.2 reduce-scatter.107
  1395.4 60.7 reduce-scatter.103
  1458.4 19.6 reduce-scatter.127
  1480.3 17.1 reduce-scatter.125
  1499.7 17.7 reduce-scatter.123
  1519.6 17.8 reduce-scatter.121
  1540.3 17.9 reduce-scatter.119
  1560.9 17.1 reduce-scatter.115
  1580.3 17.0 reduce-scatter.117
  1600.2 17.7 reduce-scatter.113
  1620.7 17.9 reduce-scatter.111
  1641.2 84.7 all-reduce.4
  (4 shorter events, 57.9 us)
